TPU v7x, 128 devices: a whole 4x4x4 slice. The times are simulated.
128 devices in a mesh: dp: 4 (over z), ctx: 32 (over y, x, core).
Axes of the slice: x: 4, y: 4, z: 4, core: 2. Of those that a mesh axis runs over, the one named last changes fastest.
Arguments:
- source_picture_sequence: bfloat16 [4, 128, 8, 8, 16, 128], P('dp', 'ctx'), may hold values from -6 to 6
- slot_assignment: int32 [128], replicated, may hold values from 0 to 127, as said below
- segment_piece_counts: int32 [16], replicated, may hold values from 1 to 16, 128 in all
- logit_scaling: float32 [4], replicated, may hold values from 1 to 16
- filter_tap_coefficients: bfloat16 [3456, 256], replicated, may hold values from -0.109375 to 0.109375
- triple_linear_matrix: bfloat16 [256, 768], replicated, may hold values from -0.375 to 0.375
- final_linear_matrix: bfloat16 [256, 256], replicated, may hold values from -0.375 to 0.375
- upstream_gradient: bfloat16 [4, 128, 4, 128, 256], P('dp', 'ctx'), may hold values from -6 to 6
Outputs:
- latents: bfloat16 [4, 128, 4, 128, 256], P('dp', 'ctx')
- conv_grad: float32 [3456, 256], P('ctx')
Inputs may be any that keep to these rules, and one draw needn't show every extreme that they name: `slot_assignment`: A permutation of the span numbers; entry i names the span at slot i, held by device i // 4. Each quarter of the span numbers, in order, fills one of the 4 positions on every device. The spans that follow one device's spans lie on at most two devices, at most two on any one device, and so do the spans that precede them; in every draw some device has two spans followed by spans on one other device.
All inputs are finite; a program needn't handle non-finite values.
Results may differ from a plain program's by a relative error of at most 0.0058.
Values may be sent and summed in bfloat16 or wider, within the bound.
A program may use at most 128 MiB of HBM per device.

v0:
```python
import jax
import jax.numpy as jnp
from jax import lax
from jax.sharding import PartitionSpec as P

masked_score = -1e30


def clip_marks(segment_piece_counts, span_ids):
    clip_ends = jnp.cumsum(segment_piece_counts, dtype=jnp.int32)
    clip_starts = clip_ends - segment_piece_counts
    clip_index = jnp.sum(
        (span_ids[:, None] >= clip_ends[None, :]).astype(jnp.int32), axis=1, dtype=jnp.int32
    )
    opening = jnp.any(span_ids[:, None] == clip_starts[None, :], axis=1)
    return (clip_index, opening)


def locate(span_ids, slot_assignment):
    slot_ids = jnp.arange(slot_assignment.shape[0], dtype=jnp.int32)
    matches = slot_assignment[None, :] == span_ids[:, None]
    return jnp.sum(jnp.where(matches, slot_ids[None, :], 0), axis=1, dtype=jnp.int32)


def conv_patches(frames):
    span_total, unused_len, rows_h, cols_w, channel_in = frames.shape
    padded = jnp.pad(frames, ((0, 0), (0, 0), (1, 1), (1, 1), (0, 0)))
    tap_list = []
    for step_t in range(3):
        for step_h in range(3):
            for step_w in range(3):
                tap_list.append(
                    padded[
                        :,
                        step_t : step_t + 7 : 2,
                        step_h : step_h + rows_h,
                        step_w : step_w + cols_w,
                        :,
                    ]
                )
    return jnp.concatenate(tap_list, axis=-1).reshape(-1, 27 * channel_in)


def timewise_softmax_mixing(
    grid_tile_entries, logit_scaling, triple_linear_matrix, final_linear_matrix, allowance_pattern
):
    channel_width = grid_tile_entries.shape[-1]
    channel_group_index = logit_scaling.shape[0]
    head_size = channel_width // channel_group_index
    values32 = grid_tile_entries.astype(jnp.float32)
    normed = (
        values32 * lax.rsqrt(jnp.mean(values32 * values32, axis=-1, keepdims=True) + 1e-06)
    ).astype(jnp.bfloat16)
    projected = jnp.einsum(
        "gac,cd->gad", normed, triple_linear_matrix, preferred_element_type=jnp.float32
    )
    head_shape = grid_tile_entries.shape[:2] + (channel_group_index, head_size)
    queries = projected[..., :channel_width].reshape(head_shape)
    keys_all = projected[..., channel_width : 2 * channel_width].reshape(head_shape)
    head_values = projected[..., 2 * channel_width :].reshape(head_shape).astype(jnp.bfloat16)
    queries = queries * lax.rsqrt(jnp.sum(queries * queries, axis=-1, keepdims=True) + 1e-06)
    keys_all = keys_all * lax.rsqrt(jnp.sum(keys_all * keys_all, axis=-1, keepdims=True) + 1e-06)
    affinity_logits = jnp.einsum(
        "gahd,gbhd->ghab", queries, keys_all, precision=lax.Precision.HIGHEST
    )
    affinity_logits = affinity_logits * logit_scaling[None, :, None, None]
    affinity_logits = jnp.where(allowance_pattern[None, None], affinity_logits, masked_score)
    highest = jnp.max(affinity_logits, axis=-1, keepdims=True)
    weights = jnp.exp(affinity_logits - highest)
    probabilities = (weights / jnp.sum(weights, axis=-1, keepdims=True)).astype(jnp.bfloat16)
    mixed_heads = jnp.einsum(
        "ghab,gbhd->gahd", probabilities, head_values, preferred_element_type=jnp.float32
    )
    mixed_heads = mixed_heads.astype(jnp.bfloat16).reshape(grid_tile_entries.shape)
    branch = jnp.einsum(
        "gac,cd->gad", mixed_heads, final_linear_matrix, preferred_element_type=jnp.float32
    )
    return (values32 + branch).astype(jnp.bfloat16)


def per_device(
    source_picture_sequence,
    slot_assignment,
    segment_piece_counts,
    logit_scaling,
    filter_tap_coefficients,
    triple_linear_matrix,
    final_linear_matrix,
    upstream_gradient,
):
    my_index = lax.axis_index("ctx")
    local_frames = source_picture_sequence[0]
    slot_count = local_frames.shape[0]
    my_spans = lax.dynamic_slice_in_dim(slot_assignment, my_index * slot_count, slot_count)
    unused_clip, opening = clip_marks(segment_piece_counts, my_spans)
    pred_slot = locate(jnp.maximum(my_spans - 1, 0), slot_assignment)
    tails = local_frames[:, 6:]
    shard_rows = lax.all_gather(tails, "ctx", axis=0, tiled=True)
    inside = (pred_slot >= 0) & (pred_slot < shard_rows.shape[0])
    chosen = shard_rows[jnp.clip(pred_slot, 0, shard_rows.shape[0] - 1)]
    previous = jnp.where(inside[:, None, None, None, None], chosen, jnp.zeros_like(tails))
    previous = jnp.where(opening[:, None, None, None, None], jnp.zeros_like(previous), previous)
    patches = conv_patches(jnp.concatenate([previous, local_frames], axis=1))
    channels = filter_tap_coefficients.shape[1]
    cell_count = local_frames.shape[2] * local_frames.shape[3]
    conv_out = jnp.dot(patches, filter_tap_coefficients, preferred_element_type=jnp.float32).astype(
        jnp.bfloat16
    )
    conv_out = conv_out.reshape(slot_count, 4, cell_count, channels)
    grad_rows = upstream_gradient[0].reshape(-1, channels)
    grad_share = lax.psum_scatter(
        jnp.dot(patches.T, grad_rows, preferred_element_type=jnp.float32),
        "ctx",
        scatter_dimension=0,
        tiled=True,
    )
    conv_grad = lax.psum(grad_share, "dp")
    gathered = lax.all_to_all(conv_out, "ctx", split_axis=2, concat_axis=0, tiled=True)
    frame_total = gathered.shape[0] * 4
    cells_dev = gathered.shape[2]
    location_entry_count = jnp.transpose(
        gathered.reshape(frame_total, cells_dev, channels), (1, 0, 2)
    )
    clip_all, unused_open = clip_marks(segment_piece_counts, slot_assignment)
    frame_clip = jnp.repeat(clip_all, 4)
    frame_time = (slot_assignment[:, None] * 4 + jnp.arange(4, dtype=jnp.int32)[None, :]).reshape(
        -1
    )
    allowance_pattern = (frame_clip[:, None] == frame_clip[None, :]) & (
        frame_time[None, :] <= frame_time[:, None]
    )
    cell_group = 1
    block_list = location_entry_count.reshape(
        cells_dev // cell_group, cell_group, frame_total, channels
    )
    blended_result = lax.map(
        lambda grid_tile_entries: timewise_softmax_mixing(
            grid_tile_entries,
            logit_scaling,
            triple_linear_matrix,
            final_linear_matrix,
            allowance_pattern,
        ),
        block_list,
    )
    blended_result = jnp.transpose(
        blended_result.reshape(cells_dev, frame_total, channels), (1, 0, 2)
    ).reshape(gathered.shape)
    latents = lax.all_to_all(blended_result, "ctx", split_axis=0, concat_axis=2, tiled=True)
    return (latents[None], conv_grad)


def solution(mesh):
    placed = (
        P("dp", "ctx", None, None, None, None),
        P(),
        P(),
        P(),
        P(),
        P(),
        P(),
        P("dp", "ctx", None, None, None),
    )
    return jax.shard_map(
        per_device,
        mesh=mesh,
        in_specs=placed,
        out_specs=(P("dp", "ctx", None, None, None), P("ctx", None)),
        check_vma=False,
    )
```

profile of v0, /device:TPU:0, one launch (start us, length us, event | category | flops | bytes accessed | tf_op | source)
XLA Modules:
  0.0 376.9 jit_solution(8046809622749582942)
XLA Ops:
  14.2 51.2 %all-gather.2.cloned.1.call-done = bf16[128,2,8,16,128]{4,3,2,1,0:T(8,128)(2,1)} async-done(((bf16[4,2,8,16,128]{4,3,2,1,0:T(8,128)(2,1)}), bf16[128,2,8,16,128]{4,3,2,1,0:T(8,128)(2,1)}) %all-gather.2.cloned.1.call-update) | async-done | bytes 8388624 | tf_op jit(solution)/shard_map/all_gather | solution.py:98
  65.4 4.0 %gather_fusion = bf16[4,2,8,16,128]{4,3,2,1,0:T(8,128)(2,1)S(1)} fusion(bf16[128,2,8,16,128]{4,3,2,1,0:T(8,128)(2,1)} %all-gather.2.cloned.1.call-done, s32[1024]{0:T(1024)S(1)} %pad_clamp_fusion), kind=kCustom, calls=%fused_computation | custom fusion | bytes 524304 | tf_op jit(solution)/shard_map/gather | solution.py:100
  78.5 4.1 %convolution_convert_fusion = bf16[2048,256]{1,0:T(8,128)(2,1)S(1)} fusion(bf16[2048,3456]{1,0:T(8,128)(2,1)S(1)} %bitcast.102, bf16[3456,256]{1,0:T(8,128)(2,1)S(1)} %copy-done), kind=kOutput, calls=%fused_computation.47 | convolution fusion | flops 3624402944 | bytes 16973824 | tf_op jit(solution)/shard_map/dot_general | solution.py:106
  85.3 5.6 %all-to-all-start = ((bf16[4,4,128,256]{3,1,0,2:T(4,128)(2,1)}), bf16[4,4,128,256]{3,1,0,2:T(4,128)(2,1)S(1)}, u32[]{:S(2)}, u32[]{:S(2)}) async-start(bf16[4,4,128,256]{3,1,0,2:T(4,128)(2,1)} %copy.55), calls=%async_computation | async-start | bytes 2097152 | tf_op jit(solution)/shard_map/all_to_all | solution.py:118
  91.0 10.9 %fusion.36 = f32[3456,256]{1,0:T(8,128)} fusion(bf16[2048,3456]{1,0:T(8,128)(2,1)} %bitcast.103, bf16[2048,256]{1,0:T(8,128)(2,1)} %bitcast.105), kind=kOutput, calls=%fused_computation.91 | convolution fusion | flops 3623878656 | bytes 18743296 | tf_op jit(solution)/shard_map/dot_general | solution.py:112
  101.9 6.1 %all-to-all-done = bf16[4,4,128,256]{3,1,0,2:T(4,128)(2,1)S(1)} async-done(((bf16[4,4,128,256]{3,1,0,2:T(4,128)(2,1)}), bf16[4,4,128,256]{3,1,0,2:T(4,128)(2,1)S(1)}, u32[]{:S(2)}, u32[]{:S(2)}) %all-to-all-start) | async-done | bytes 1048608 | tf_op jit(solution)/shard_map/all_to_all | solution.py:118
  109.4 2.1 reshape.266
  111.6 120.4 %while.11 = (s32[]{:T(128)}, bf16[4,1,512,256]{3,2,1,0:T(8,128)(2,1)}, bf16[4,1,512,256]{3,2,1,0:T(8,128)(2,1)}, bf16[256,768]{1,0:T(8,128)(2,1)}, f32[4]{0:T(12...) while((s32[]{:T(128)}, ...), condition=%wide.region_10.11_spmd.clone, body=%wide.region_4.10_spmd.clone.sunk | while | flops 1219232768 | bytes 31814784 | solution.py:136
  118.8 2.1 copy.71
  121.9 2.1 copy.68
  126.1 4.7 %fusion.65 = f32[4,512,512]{1,2,0:T(8,128)S(1)} fusion(f32[512,4,64]{0,2,1:T(8,128)} %bitcast.89, f32[512,4,64]{0,2,1:T(8,128)} %bitcast.90, f32[512,4]{0,1:T(4,128)S(1)} %get-tuple-element.153, f32[512,4]{0,1:T(4,128)S(1)} %get-tuple-element.154), kind=kOutput, calls=%fused_computation.24.clone.1 | convolution fusion | flops 805568512 | bytes 5259264 | tf_op jit(solution)/shard_map/while/body/eval_jaxpr/gahd,gbhd->ghab/dot_general | solution.py:63
  131.1 4.2 %fusion.66 = (f32[4,512]{1,0:T(4,128)S(1)}, f32[4,512,512]{1,2,0:T(8,128)}) fusion(f32[4,512,512]{1,2,0:T(8,128)S(1)} %fusion.65, f32[4]{0:T(128)S(1)} %get-tuple-element.181, pred[512,512]{0,1:T(8,128)(4,1)S(1)} %compare_and_fusion.3), kind=kOutput, calls=%fused_computation.90.clone.1 | output fusion | flops 6291967 | bytes 8658960 | tf_op jit(solution)/shard_map/while/body/eval_jaxpr/sub | solution.py:69
  137.0 2.7 fusion.67
  148.9 2.1 copy.71
  152.0 2.1 copy.68
  156.1 4.7 %fusion.65 = f32[4,512,512]{1,2,0:T(8,128)S(1)} fusion(f32[512,4,64]{0,2,1:T(8,128)} %bitcast.89, f32[512,4,64]{0,2,1:T(8,128)} %bitcast.90, f32[512,4]{0,1:T(4,128)S(1)} %get-tuple-element.153, f32[512,4]{0,1:T(4,128)S(1)} %get-tuple-element.154), kind=kOutput, calls=%fused_computation.24.clone.1 | convolution fusion | flops 805568512 | bytes 5259264 | tf_op jit(solution)/shard_map/while/body/eval_jaxpr/gahd,gbhd->ghab/dot_general | solution.py:63
  161.2 4.2 %fusion.66 = (f32[4,512]{1,0:T(4,128)S(1)}, f32[4,512,512]{1,2,0:T(8,128)}) fusion(f32[4,512,512]{1,2,0:T(8,128)S(1)} %fusion.65, f32[4]{0:T(128)S(1)} %get-tuple-element.181, pred[512,512]{0,1:T(8,128)(4,1)S(1)} %compare_and_fusion.3), kind=kOutput, calls=%fused_computation.90.clone.1 | output fusion | flops 6291967 | bytes 8658960 | tf_op jit(solution)/shard_map/while/body/eval_jaxpr/sub | solution.py:69
  167.1 2.7 fusion.67
  179.0 2.1 copy.71
  182.1 2.1 copy.68
  186.2 4.7 %fusion.65 = f32[4,512,512]{1,2,0:T(8,128)S(1)} fusion(f32[512,4,64]{0,2,1:T(8,128)} %bitcast.89, f32[512,4,64]{0,2,1:T(8,128)} %bitcast.90, f32[512,4]{0,1:T(4,128)S(1)} %get-tuple-element.153, f32[512,4]{0,1:T(4,128)S(1)} %get-tuple-element.154), kind=kOutput, calls=%fused_computation.24.clone.1 | convolution fusion | flops 805568512 | bytes 5259264 | tf_op jit(solution)/shard_map/while/body/eval_jaxpr/gahd,gbhd->ghab/dot_general | solution.py:63
  191.2 4.2 %fusion.66 = (f32[4,512]{1,0:T(4,128)S(1)}, f32[4,512,512]{1,2,0:T(8,128)}) fusion(f32[4,512,512]{1,2,0:T(8,128)S(1)} %fusion.65, f32[4]{0:T(128)S(1)} %get-tuple-element.181, pred[512,512]{0,1:T(8,128)(4,1)S(1)} %compare_and_fusion.3), kind=kOutput, calls=%fused_computation.90.clone.1 | output fusion | flops 6291967 | bytes 8658960 | tf_op jit(solution)/shard_map/while/body/eval_jaxpr/sub | solution.py:69
  197.2 2.7 fusion.67
  209.0 2.1 copy.71
  212.2 2.1 copy.68
  216.3 4.7 %fusion.65 = f32[4,512,512]{1,2,0:T(8,128)S(1)} fusion(f32[512,4,64]{0,2,1:T(8,128)} %bitcast.89, f32[512,4,64]{0,2,1:T(8,128)} %bitcast.90, f32[512,4]{0,1:T(4,128)S(1)} %get-tuple-element.153, f32[512,4]{0,1:T(4,128)S(1)} %get-tuple-element.154), kind=kOutput, calls=%fused_computation.24.clone.1 | convolution fusion | flops 805568512 | bytes 5259264 | tf_op jit(solution)/shard_map/while/body/eval_jaxpr/gahd,gbhd->ghab/dot_general | solution.py:63
  221.3 4.2 %fusion.66 = (f32[4,512]{1,0:T(4,128)S(1)}, f32[4,512,512]{1,2,0:T(8,128)}) fusion(f32[4,512,512]{1,2,0:T(8,128)S(1)} %fusion.65, f32[4]{0:T(128)S(1)} %get-tuple-element.181, pred[512,512]{0,1:T(8,128)(4,1)S(1)} %compare_and_fusion.3), kind=kOutput, calls=%fused_computation.90.clone.1 | output fusion | flops 6291967 | bytes 8658960 | tf_op jit(solution)/shard_map/while/body/eval_jaxpr/sub | solution.py:69
  227.3 2.7 fusion.67
  231.9 3.0 copy.61
  235.0 3.9 %all-to-all-start.1 = ((bf16[128,4,4,256]{3,2,1,0:T(4,128)(2,1)}), bf16[128,4,4,256]{3,2,1,0:T(4,128)(2,1)S(1)}, u32[]{:S(2)}, u32[]{:S(2)}) async-start(bf16[128,4,4,256]{3,2,1,0:T(4,128)(2,1)} %bitcast.95), calls=%async_computation.1 | async-start | bytes 2097152 | tf_op jit(solution)/shard_map/all_to_all | solution.py:149
  238.9 84.1 %fusion.2 = f32[112,256]{1,0:T(8,128)S(1)} fusion(f32[3456,256]{1,0:T(8,128)} %fusion.36), kind=kCustom, calls=%all-reduce-scatter | all-reduce-scatter fusion | flops 917505 | bytes 3654144
  329.8 38.7 %all-reduce.5.cloned.1.call-done = f32[108,256]{1,0:T(8,128)} async-done(((f32[108,256]{1,0:T(8,128)}), f32[108,256]{1,0:T(8,128)}) %all-reduce.5.cloned.1.call-update) | async-done | bytes 110608 | tf_op jit(solution)/shard_map/psum | solution.py:117
  (127 shorter events, 85.1 us)
Async XLA Ops:
  7.2 71.3 %copy-start = (bf16[3456,256]{1,0:T(8,128)(2,1)S(1)}, bf16[3456,256]{1,0:T(8,128)(2,1)}, u32[]{:S(2)}) copy-start(bf16[3456,256]{1,0:T(8,128)(2,1)} %param.14) | copy-start | bytes 5308420
  7.2 58.2 %all-gather.2.cloned.1.call-start = ((), (), s32[]{:S(2)}) async-start(), calls=%async_computation.2 | async-start | bytes 8650752 | tf_op jit(solution)/shard_map/all_gather | solution.py:98
  78.5 5.1 %copy-start.1 = (bf16[4,4,8,16,3456]{4,3,2,1,0:T(8,128)(2,1)}, bf16[4,4,8,16,3456]{4,3,2,1,0:T(8,128)(2,1)S(1)}, u32[]{:S(2)}) copy-start(bf16[4,4,8,16,3456]{4,3,2,1,0:T(8,128)(2,1)S(1)} %slice_dynamic-update-slice_fusion) | copy-start | bytes 42467332
  85.3 22.7 %all-to-all-start = ((bf16[4,4,128,256]{3,1,0,2:T(4,128)(2,1)}), bf16[4,4,128,256]{3,1,0,2:T(4,128)(2,1)S(1)}, u32[]{:S(2)}, u32[]{:S(2)}) async-start(bf16[4,4,128,256]{3,1,0,2:T(4,128)(2,1)} %copy.55), calls=%async_computation | async-start | bytes 2097152 | tf_op jit(solution)/shard_map/all_to_all | solution.py:118
  91.0 20.6 %copy-start.3 = (bf16[256,256]{1,0:T(8,128)(2,1)S(1)}, bf16[256,256]{1,0:T(8,128)(2,1)}, u32[]{:S(2)}) copy-start(bf16[256,256]{1,0:T(8,128)(2,1)} %param.16) | copy-start | bytes 393220
  91.0 20.6 %copy-start.4 = (f32[4]{0:T(128)S(1)}, f32[4]{0:T(128)}, u32[]{:S(2)}) copy-start(f32[4]{0:T(128)} %param.13) | copy-start | bytes 52
  111.5 214.1 %copy-start.2 = (u32[128]{0:T(128)S(1)}, u32[128]{0:T(128)}, u32[]{:S(2)}) copy-start(u32[128]{0:T(128)} %constant.55) | copy-start | bytes 1540
  235.0 93.2 %all-to-all-start.1 = ((bf16[128,4,4,256]{3,2,1,0:T(4,128)(2,1)}), bf16[128,4,4,256]{3,2,1,0:T(4,128)(2,1)S(1)}, u32[]{:S(2)}, u32[]{:S(2)}) async-start(bf16[128,4,4,256]{3,2,1,0:T(4,128)(2,1)} %bitcast.95), calls=%async_computation.1 | async-start | bytes 2097152 | tf_op jit(solution)/shard_map/all_to_all | solution.py:149
  238.9 129.6 %all-reduce.5.cloned.1.call-start = ((), (), s32[]{:S(2)}) async-start(), calls=%async_computation.3 | async-start | bytes 229376 | tf_op jit(solution)/shard_map/psum | solution.py:117
  323.0 4.0 %collective-permute-start = (f32[112,256]{1,0:T(8,128)S(1)}, f32[112,256]{1,0:T(8,128)S(1)}, u32[]{:S(2)}, u32[]{:S(2)}) collective-permute-start(f32[112,256]{1,0:T(8,128)S(1)} %fusion.2), channel_id=1, source_target_pairs={{0,1},{1,2},{2,3},{3,4},{4,5},{5,6},{6,7},{7,8},{8,9},{9,10},{10,1... | collective-permute-start | bytes 344072
  324.3 2.7 collective-permute-start.1
Sparse Core Ops, SparseCore 0:
  10.3 55.1 all-gather.1
  328.3 40.1 all-reduce.4
where the time goes:
time: 379 us; the launch traced here: 377 us
  waiting for transfers between devices  96.2 us (25%)
  blocking collectives  84.1 us (22%)
  local copies, waits for them, and re-layouts  67.8 us (18%)
  matrix products  58.3 us (15%)
  other arithmetic  42.9 us (11%)
  between operations  15.1 us (4%)
  starting transfers between devices  12.2 us (3%)
    unnamed x1, blocking collectives  84.1 us
    all_gather x1, waiting for transfers between devices, per_device(): shard_rows = lax.all_gather(tails, 'ctx', axis=0, tiled=True)  51.2 us
    psum x1, waiting for transfers between devices, per_device(): conv_grad = lax.psum(grad_share, 'dp')  38.7 us
    dot_general x4, matrix products, timewise_softmax_mixing(): jnp.einsum('gahd,gbhd->ghab', queries, keys_all, precision=lax.Precision....  18.9 us
    sub x4, other arithmetic, timewise_softmax_mixing(): weights = jnp.exp(affinity_logits - highest)  16.6 us
    unnamed x42, local copies, waits for them, and re-layouts  11.7 us
    dot_general x1, matrix products, per_device(): jnp.dot(patches.T, grad_rows, preferred_element_type=jnp.float32)  10.9 us
    dot_general x4, matrix products, timewise_softmax_mixing(): jnp.einsum('ghab,gbhd->gahd', probabilities, head_values, preferred_eleme...  10.7 us
  transfers between devices with their start and end apart: 6, of which 4 were waited for; matrix products, arithmetic and copies ran while one was open for 27% of the time, Pallas kernels for 0%

commit v1 on v0

--- a/solution.py
+++ b/solution.py
@@ -95,7 +95,9 @@
     unused_clip, opening = clip_marks(segment_piece_counts, my_spans)
     pred_slot = locate(jnp.maximum(my_spans - 1, 0), slot_assignment)
     tails = local_frames[:, 6:]
-    shard_rows = lax.all_gather(tails, "ctx", axis=0, tiled=True)
+    shard_rows = jnp.concatenate(
+        lax.all_to_all(jnp.stack(lax.psum(1, "ctx") * [tails]), "ctx", 0, 0), axis=0
+    )
     inside = (pred_slot >= 0) & (pred_slot < shard_rows.shape[0])
     chosen = shard_rows[jnp.clip(pred_slot, 0, shard_rows.shape[0] - 1)]
     previous = jnp.where(inside[:, None, None, None, None], chosen, jnp.zeros_like(tails))

time: 379 us -> 395 us (1.042)
  waiting for transfers between devices: 96.2 us -> 152 us
  local copies, waits for them, and re-layouts: 67.8 us -> 41.9 us
  other arithmetic: 42.9 us -> 29.3 us
  matrix products: 58.3 us -> 51.6 us
  starting transfers between devices: 12.2 us -> 18.4 us
    all_to_all x0 -> x1, waiting for transfers between devices: none -> 105 us  [per_device(): lax.all_to_all(jnp.stack(lax.psum(1, 'ctx') * [tails]), 'ctx', 0, 0)]
    all_gather x1 -> x0, waiting for transfers between devices: 51.2 us -> none  [per_device(): shard_rows = lax.all_gather(tails, 'ctx', axis=0, tiled=True)]
    all_to_all x0 -> x1, starting transfers between devices: none -> 7.69 us  [per_device(): lax.all_to_all(jnp.stack(lax.psum(1, 'ctx') * [tails]), 'ctx', 0, 0)]
    slice x4, local copies, waits for them, and re-layouts: 8.24 us -> 0.79 us  [timewise_softmax_mixing(): projected[..., channel_width:2 * channel_width].reshape(head_shape)]
    slice x4, local copies, waits for them, and re-layouts: 8.21 us -> 0.79 us  [timewise_softmax_mixing(): queries = projected[..., :channel_width].reshape(head_shape)]
    slice x8, local copies, waits for them, and re-layouts: 7.29 us -> 0.67 us  [timewise_softmax_mixing(): projected[..., 2 * channel_width:].reshape(head_shape).astype(jnp.bfloat16)]
    dot_general x4, matrix products: 18.9 us -> 14.1 us  [timewise_softmax_mixing(): jnp.einsum('gahd,gbhd->ghab', queries, keys_all, precision=lax.Precision....]
    another operation x1 -> x2, local copies, waits for them, and re-layouts: 0.73 us -> 5.42 us  [the longest x1 5.34 us: per_device(): jnp.stack(lax.psum(1, 'ctx') * [tails])]
  transfers between devices with their start and end apart: 6 -> 6, of which waited for: 4 -> 4; matrix products, arithmetic and copies ran while one was open for 27% -> 25% of each run, Pallas kernels for 0% -> 0%
where the time goes in v1:
time: 395 us; the launch traced here: 393 us
  waiting for transfers between devices  152 us (38%)
  blocking collectives  84.1 us (21%)
  matrix products  51.6 us (13%)
  local copies, waits for them, and re-layouts  41.9 us (11%)
  other arithmetic  29.3 us (7%)
  starting transfers between devices  18.4 us (5%)
  between operations  15.1 us (4%)
    all_to_all x1, waiting for transfers between devices, per_device(): lax.all_to_all(jnp.stack(lax.psum(1, 'ctx') * [tails]), 'ctx', 0, 0)  105 us
    unnamed x1, blocking collectives  84.1 us
    psum x1, waiting for transfers between devices, per_device(): conv_grad = lax.psum(grad_share, 'dp')  39.6 us
    sub x4, other arithmetic, timewise_softmax_mixing(): weights = jnp.exp(affinity_logits - highest)  16.6 us
    dot_general x4, matrix products, timewise_softmax_mixing(): jnp.einsum('gahd,gbhd->ghab', queries, keys_all, precision=lax.Precision....  14.1 us
    unnamed x52, local copies, waits for them, and re-layouts  11.7 us
    dot_general x4, matrix products, timewise_softmax_mixing(): jnp.einsum('ghab,gbhd->gahd', probabilities, head_values, preferred_eleme...  10.7 us
    dot_general x1, matrix products, per_device(): jnp.dot(patches.T, grad_rows, preferred_element_type=jnp.float32)  8.91 us
  transfers between devices with their start and end apart: 6, of which 4 were waited for; matrix products, arithmetic and copies ran while one was open for 25% of the time, Pallas kernels for 0%

profile of v1, /device:TPU:0, one launch (start us, length us, event | category | flops | bytes accessed | tf_op | source)
XLA Modules:
  0.0 393.2 jit_solution(14491223263736302168)
XLA Ops:
  8.3 5.3 %stack.2 = bf16[32,4,2,8,16,128]{5,4,3,2,1,0:T(8,128)(2,1)} broadcast(bf16[4,2,8,16,128]{4,3,2,1,0:T(8,128)(2,1)S(1)} %slice.130), dimensions={1,2,3,4,5} | broadcast | bytes 8650752 | tf_op jit(solution)/shard_map/stack | solution.py:99
  13.6 7.7 %all-to-all-start = ((bf16[32,4,2,8,16,128]{5,4,3,2,1,0:T(8,128)(2,1)}), bf16[32,4,2,8,16,128]{5,4,3,2,1,0:T(8,128)(2,1)}, u32[]{:S(2)}, u32[]{:S(2)}) async-start(bf16[32,4,2,8,16,128]{5,4,3,2,1,0:T(8,128)(2,1)} %stack.2), calls=%async_computation | async-start | bytes 16777216 | tf_op jit(solution)/shard_map/all_to_all | solution.py:99
  22.6 104.6 %all-to-all-done = bf16[32,4,2,8,16,128]{5,4,3,2,1,0:T(8,128)(2,1)} async-done(((bf16[32,4,2,8,16,128]{5,4,3,2,1,0:T(8,128)(2,1)}), bf16[32,4,2,8,16,128]{5,4,3,2,1,0:T(8,128)(2,1)}, u32[]{:S(2)}, u32[]{:S(2)}) %all-to-all-start) | async-done | bytes 8388640 | tf_op jit(solution)/shard_map/all_to_all | solution.py:99
  127.2 4.0 %gather_fusion = bf16[4,2,8,16,128]{4,3,2,1,0:T(8,128)(2,1)S(1)} fusion(bf16[128,2,8,16,128]{4,3,2,1,0:T(8,128)(2,1)} %bitcast.2, s32[1024]{0:T(1024)S(1)} %pad_clamp_fusion), kind=kCustom, calls=%fused_computation | custom fusion | bytes 524304 | tf_op jit(solution)/shard_map/gather | solution.py:102
  139.4 4.1 %convolution_convert_fusion = bf16[2048,256]{1,0:T(8,128)(2,1)S(1)} fusion(bf16[2048,3456]{1,0:T(8,128)(2,1)S(1)} %bitcast.103, bf16[3456,256]{1,0:T(8,128)(2,1)S(1)} %copy-done), kind=kOutput, calls=%fused_computation.47 | convolution fusion | flops 3624402944 | bytes 16973824 | tf_op jit(solution)/shard_map/dot_general | solution.py:108
  144.4 1.8 copy.55
  146.2 4.1 %all-to-all-start.1 = ((bf16[4,4,128,256]{3,1,0,2:T(4,128)(2,1)}), bf16[4,4,128,256]{3,1,0,2:T(4,128)(2,1)S(1)}, u32[]{:S(2)}, u32[]{:S(2)}) async-start(bf16[4,4,128,256]{3,1,0,2:T(4,128)(2,1)} %copy.55), calls=%async_computation.1 | async-start | bytes 2097152 | tf_op jit(solution)/shard_map/all_to_all | solution.py:120
  150.4 8.9 %fusion.36 = f32[3456,256]{1,0:T(8,128)} fusion(bf16[2048,3456]{1,0:T(8,128)(2,1)} %bitcast.104, bf16[2048,256]{1,0:T(8,128)(2,1)S(1)} %bitcast.106), kind=kOutput, calls=%fused_computation.91 | convolution fusion | flops 3623878656 | bytes 18743296 | tf_op jit(solution)/shard_map/dot_general | solution.py:114
  159.3 8.0 %all-to-all-done.1 = bf16[4,4,128,256]{3,1,0,2:T(4,128)(2,1)S(1)} async-done(((bf16[4,4,128,256]{3,1,0,2:T(4,128)(2,1)}), bf16[4,4,128,256]{3,1,0,2:T(4,128)(2,1)S(1)}, u32[]{:S(2)}, u32[]{:S(2)}) %all-to-all-start.1) | async-done | bytes 1048608 | tf_op jit(solution)/shard_map/all_to_all | solution.py:120
  168.9 78.3 %while.11 = (s32[]{:T(128)}, bf16[4,1,512,256]{3,2,1,0:T(8,128)(2,1)}, bf16[4,1,512,256]{3,2,1,0:T(8,128)(2,1)}, bf16[256,768]{1,0:T(8,128)(2,1)}, f32[4]{0:T(12...) while((s32[]{:T(128)}, ...), condition=%wide.region_10.11_spmd.clone, body=%wide.region_4.10_spmd.clone.sunk | while | flops 1219232768 | bytes 31814784 | solution.py:138
  170.0 1.5 convolution_bitcast_fusion.2
  175.7 3.5 fusion.65
  179.6 4.2 %fusion.66 = (f32[4,512]{1,0:T(4,128)S(1)}, f32[4,512,512]{1,2,0:T(8,128)}) fusion(f32[4,512,512]{1,2,0:T(8,128)S(1)} %fusion.65, f32[4]{0:T(128)S(1)} %get-tuple-element.181, pred[512,512]{0,1:T(8,128)(4,1)S(1)} %compare_and_fusion.3), kind=kOutput, calls=%fused_computation.90.clone.1 | output fusion | flops 6291967 | bytes 8658960 | tf_op jit(solution)/shard_map/while/body/eval_jaxpr/sub | solution.py:69
  183.9 2.7 fusion.67
  186.6 1.9 fusion.68
  195.3 3.5 fusion.65
  199.1 4.2 %fusion.66 = (f32[4,512]{1,0:T(4,128)S(1)}, f32[4,512,512]{1,2,0:T(8,128)}) fusion(f32[4,512,512]{1,2,0:T(8,128)S(1)} %fusion.65, f32[4]{0:T(128)S(1)} %get-tuple-element.181, pred[512,512]{0,1:T(8,128)(4,1)S(1)} %compare_and_fusion.3), kind=kOutput, calls=%fused_computation.90.clone.1 | output fusion | flops 6291967 | bytes 8658960 | tf_op jit(solution)/shard_map/while/body/eval_jaxpr/sub | solution.py:69
  203.5 2.7 fusion.67
  206.1 1.9 fusion.68
  214.9 3.5 fusion.65
  218.7 4.2 %fusion.66 = (f32[4,512]{1,0:T(4,128)S(1)}, f32[4,512,512]{1,2,0:T(8,128)}) fusion(f32[4,512,512]{1,2,0:T(8,128)S(1)} %fusion.65, f32[4]{0:T(128)S(1)} %get-tuple-element.181, pred[512,512]{0,1:T(8,128)(4,1)S(1)} %compare_and_fusion.3), kind=kOutput, calls=%fused_computation.90.clone.1 | output fusion | flops 6291967 | bytes 8658960 | tf_op jit(solution)/shard_map/while/body/eval_jaxpr/sub | solution.py:69
  223.0 2.7 fusion.67
  225.7 1.9 fusion.68
  234.5 3.5 fusion.65
  238.3 4.2 %fusion.66 = (f32[4,512]{1,0:T(4,128)S(1)}, f32[4,512,512]{1,2,0:T(8,128)}) fusion(f32[4,512,512]{1,2,0:T(8,128)S(1)} %fusion.65, f32[4]{0:T(128)S(1)} %get-tuple-element.181, pred[512,512]{0,1:T(8,128)(4,1)S(1)} %compare_and_fusion.3), kind=kOutput, calls=%fused_computation.90.clone.1 | output fusion | flops 6291967 | bytes 8658960 | tf_op jit(solution)/shard_map/while/body/eval_jaxpr/sub | solution.py:69
  242.6 2.7 fusion.67
  245.3 1.9 fusion.68
  247.2 3.2 copy.61
  250.4 3.9 all-to-all-start.2
  254.4 84.1 %fusion.2 = f32[112,256]{1,0:T(8,128)S(1)} fusion(f32[3456,256]{1,0:T(8,128)} %fusion.36), kind=kCustom, calls=%all-reduce-scatter | all-reduce-scatter fusion | flops 917505 | bytes 3654144
  345.2 39.6 %all-reduce.5.cloned.1.call-done = f32[108,256]{1,0:T(8,128)} async-done(((f32[108,256]{1,0:T(8,128)}), f32[108,256]{1,0:T(8,128)}) %all-reduce.5.cloned.1.call-update) | async-done | bytes 110608 | tf_op jit(solution)/shard_map/psum | solution.py:119
  384.8 1.6 copy.108
  (137 shorter events, 46.1 us)
Async XLA Ops:
  7.2 132.2 %copy-start = (bf16[3456,256]{1,0:T(8,128)(2,1)S(1)}, bf16[3456,256]{1,0:T(8,128)(2,1)}, u32[]{:S(2)}) copy-start(bf16[3456,256]{1,0:T(8,128)(2,1)} %param.14) | copy-start | bytes 5308420
  13.6 7.7 %copy-start.4 = (s32[16]{0:T(128)S(1)}, s32[16]{0:T(128)}, u32[]{:S(2)}) copy-start(s32[16]{0:T(128)} %param.12) | copy-start | bytes 196
  13.6 8.0 %copy-start.6 = (s32[128]{0:T(128)S(1)}, s32[128]{0:T(128)}, u32[]{:S(2)}) copy-start(s32[128]{0:T(128)} %param.11) | copy-start | bytes 1540
  13.6 117.7 %copy-start.2 = (bf16[1,4,8,8,16,128]{5,4,3,2,1,0:T(8,128)(2,1)S(1)}, bf16[1,4,8,8,16,128]{5,4,3,2,1,0:T(8,128)(2,1)}, u32[]{:S(2)}) copy-start(bf16[1,4,8,8,16,128]{5,4,3,2,1,0:T(8,128)(2,1)} %param.10) | copy-start | bytes 3145732
  13.6 113.6 %all-to-all-start = ((bf16[32,4,2,8,16,128]{5,4,3,2,1,0:T(8,128)(2,1)}), bf16[32,4,2,8,16,128]{5,4,3,2,1,0:T(8,128)(2,1)}, u32[]{:S(2)}, u32[]{:S(2)}) async-start(bf16[32,4,2,8,16,128]{5,4,3,2,1,0:T(8,128)(2,1)} %stack.2), calls=%async_computation | async-start | bytes 16777216 | tf_op jit(solution)/shard_map/all_to_all | solution.py:99
  139.4 5.1 %copy-start.3 = (bf16[4,4,8,16,3456]{4,3,2,1,0:T(8,128)(2,1)}, bf16[4,4,8,16,3456]{4,3,2,1,0:T(8,128)(2,1)S(1)}, u32[]{:S(2)}) copy-start(bf16[4,4,8,16,3456]{4,3,2,1,0:T(8,128)(2,1)S(1)} %slice_dynamic-update-slice_fusion) | copy-start | bytes 42467332
  139.4 11.0 %copy-start.7 = (bf16[1,4,4,128,256]{4,3,2,1,0:T(8,128)(2,1)S(1)}, bf16[1,4,4,128,256]{4,3,2,1,0:T(8,128)(2,1)}, u32[]{:S(2)}) copy-start(bf16[1,4,4,128,256]{4,3,2,1,0:T(8,128)(2,1)} %param.17) | copy-start | bytes 3145732
  146.2 21.1 %all-to-all-start.1 = ((bf16[4,4,128,256]{3,1,0,2:T(4,128)(2,1)}), bf16[4,4,128,256]{3,1,0,2:T(4,128)(2,1)S(1)}, u32[]{:S(2)}, u32[]{:S(2)}) async-start(bf16[4,4,128,256]{3,1,0,2:T(4,128)(2,1)} %copy.55), calls=%async_computation.1 | async-start | bytes 2097152 | tf_op jit(solution)/shard_map/all_to_all | solution.py:120
  150.4 18.5 %copy-start.8 = (bf16[256,256]{1,0:T(8,128)(2,1)S(1)}, bf16[256,256]{1,0:T(8,128)(2,1)}, u32[]{:S(2)}) copy-start(bf16[256,256]{1,0:T(8,128)(2,1)} %param.16) | copy-start | bytes 393220
  150.4 18.5 %copy-start.9 = (f32[4]{0:T(128)S(1)}, f32[4]{0:T(128)}, u32[]{:S(2)}) copy-start(f32[4]{0:T(128)} %param.13) | copy-start | bytes 52
  168.9 172.1 %copy-start.5 = (u32[128]{0:T(128)S(1)}, u32[128]{0:T(128)}, u32[]{:S(2)}) copy-start(u32[128]{0:T(128)} %constant.55) | copy-start | bytes 1540
  247.2 139.1 %copy-start.1 = (bf16[3456,256]{1,0:T(8,128)(2,1)S(1)}, bf16[3456,256]{1,0:T(8,128)(2,1)}, u32[]{:S(2)}) copy-start(bf16[3456,256]{1,0:T(8,128)(2,1)} %param.14) | copy-start | bytes 5308420
  250.4 93.2 %all-to-all-start.2 = ((bf16[128,4,4,256]{3,2,1,0:T(4,128)(2,1)}), bf16[128,4,4,256]{3,2,1,0:T(4,128)(2,1)S(1)}, u32[]{:S(2)}, u32[]{:S(2)}) async-start(bf16[128,4,4,256]{3,2,1,0:T(4,128)(2,1)} %bitcast.96), calls=%async_computation.2 | async-start | bytes 2097152 | tf_op jit(solution)/shard_map/all_to_all | solution.py:151
  254.3 130.5 %all-reduce.5.cloned.1.call-start = ((), (), s32[]{:S(2)}) async-start(), calls=%async_computation.3 | async-start | bytes 229376 | tf_op jit(solution)/shard_map/psum | solution.py:119
  338.4 4.0 %collective-permute-start = (f32[112,256]{1,0:T(8,128)S(1)}, f32[112,256]{1,0:T(8,128)S(1)}, u32[]{:S(2)}, u32[]{:S(2)}) collective-permute-start(f32[112,256]{1,0:T(8,128)S(1)} %fusion.2), channel_id=1, source_target_pairs={{0,1},{1,2},{2,3},{3,4},{4,5},{5,6},{6,7},{7,8},{8,9},{9,10},{10,1... | collective-permute-start | bytes 344072
  339.7 2.7 collective-permute-start.1
Sparse Core Ops, SparseCore 0:
  343.7 41.0 all-reduce.4
